TPU v7x, 1024 devices: a whole 4x8x16 slice. The times are simulated.
1024 devices in a mesh: lon: 16 (over z), lat: 4 (over x_hi, core), mem: 16 (over x_lo, y).
Axes of the slice: x: 4 (x_hi: 2, x_lo: 2; x = x_hi * 2 + x_lo), y: 8, z: 16, core: 2. Of those that a mesh axis runs over, the one named last changes fastest.
Arguments:
- controls: float32 [64, 384, 96, 128], P('mem', 'lon', 'lat'), may hold values from -6 to 6
- ensemble: bfloat16 [64, 384, 96, 128], P('mem', 'lon', 'lat'), may hold values from -1.5 to 1.5
- taps_lon: float32 [17], replicated, may hold values from 0.05 to 0.35
- taps_lat: float32 [17], replicated, may hold values from 0.05 to 0.35
- obs_columns: int32 [16, 4, 16, 16], P('lon', 'lat', 'mem'), may hold values from 0 to 575
- obs_count: int32 [16, 4, 16], P('lon', 'lat', 'mem'), may hold values from 1 to 16, as said below
- obs_quality: int32 [16, 4, 16, 16], P('lon', 'lat', 'mem'), may hold values from 0 to 3
- obs_values: float32 [16, 4, 16, 16, 128], P('lon', 'lat', 'mem'), may hold values from -6 to 6
Outputs:
- new_controls: float32 [64, 384, 96, 128], P('mem', 'lon', 'lat')
- residual: float32 [16, 4, 16, 16, 128], P('lon', 'lat', 'mem')
Inputs may be any that keep to these rules, and one draw needn't show every extreme that they name: `obs_columns`: column within the owner's tile, numbered as longitude offset times 24 plus latitude offset. `obs_count`: slots from this number on are unused; some owner has exactly 16 live slots.
All inputs are finite; a program needn't handle non-finite values.
Results may differ from a plain program's by a relative error of at most 0.0049.
Values may be sent and summed in bfloat16 or wider, within the bound.
A program may use at most 32 MiB of HBM per device.

v0:
```python
import jax
import jax.numpy as jnp
from jax import lax
from jax.sharding import PartitionSpec as P

descent = 0.5


def extended_2(x, sides, width):
    for axis, dim in sides:
        peers, length = (lax.axis_size(axis), x.shape[dim])
        up = [(i, (i + 1) % peers) for i in range(peers)]
        down = [(j, i) for i, j in up]
        last = lax.slice_in_dim(x, length - width, length, axis=dim)
        initial = lax.slice_in_dim(x, 0, width, axis=dim)
        before = lax.ppermute(last, axis, up)
        after = lax.ppermute(initial, axis, down)
        x = jnp.concatenate([before, x, after], axis=dim)
    return x


def band_matrix(kernel, row_count, flipped):
    tap_count = kernel.shape[0]
    if flipped:
        kernel = kernel[::-1]
    offset = jnp.arange(row_count + tap_count - 1)[None, :] - jnp.arange(row_count)[:, None]
    chosen = (offset[:, :, None] == jnp.arange(tap_count)[None, None, :]).astype(jnp.float32)
    return jnp.sum(chosen * kernel.astype(jnp.float32), axis=-1).astype(jnp.bfloat16)


def open_edges(extended, rim_width):
    tile_lat = extended.shape[2] - 2 * rim_width
    position = lax.axis_index("lat") * tile_lat + jnp.arange(extended.shape[2]) - rim_width
    inside = (position >= 0) & (position < lax.axis_size("lat") * tile_lat)
    return jnp.where(inside[None, None, :, None], extended, jnp.zeros((), extended.dtype))


def shards(controls, ensemble, taps_lon, taps_lat, obs_columns, obs_count, obs_quality, obs_values):
    tap_count = taps_lon.shape[0]
    rim_width = tap_count // 2
    lon_tile = controls.shape[1]
    lat_tile = controls.shape[2]
    levels = controls.shape[3]
    kernel_lon = taps_lon.astype(jnp.bfloat16)
    kernel_lat = taps_lat.astype(jnp.bfloat16)
    low = controls.astype(jnp.bfloat16)
    extended = extended_2(low, (("lon", 1), ("lat", 2)), rim_width)
    extended = open_edges(extended, rim_width)
    lon_pass = jnp.einsum(
        "ie,mejl->mijl",
        band_matrix(kernel_lon, lon_tile, False),
        extended,
        preferred_element_type=jnp.float32,
    ).astype(jnp.bfloat16)
    spread = jnp.einsum(
        "je,miel->mijl",
        band_matrix(kernel_lat, lat_tile, False),
        lon_pass,
        preferred_element_type=jnp.float32,
    )
    partial_value = jnp.sum(ensemble.astype(jnp.float32) * spread, axis=0)
    flat_part = partial_value.reshape(lon_tile * lat_tile, levels)
    columns = obs_columns[0, 0, 0]
    slot_count = columns.shape[0]
    increment = lax.psum(flat_part, "mem")
    observed = jnp.take(increment, columns, axis=0)
    active = jnp.arange(slot_count) < obs_count[0, 0, 0]
    weights = jnp.where(
        active, 0.5 * obs_quality[0, 0, 0].astype(jnp.float32), jnp.zeros((), jnp.float32)
    )
    residual = weights[:, None] * (observed - obs_values[0, 0, 0])
    empty = jnp.zeros((lon_tile * lat_tile, levels), jnp.float32)
    placed = empty.at[columns].add(residual)
    adjoint = lax.psum(placed.astype(jnp.bfloat16), "mem").astype(jnp.float32)
    adjoint = adjoint.reshape(lon_tile, lat_tile, levels)
    product = (ensemble.astype(jnp.float32) * adjoint[None]).astype(jnp.bfloat16)
    extended_back = extended_2(product, (("lon", 1), ("lat", 2)), rim_width)
    extended_back = open_edges(extended_back, rim_width)
    lat_back = jnp.einsum(
        "je,miel->mijl",
        band_matrix(kernel_lat, lat_tile, True),
        extended_back,
        preferred_element_type=jnp.float32,
    ).astype(jnp.bfloat16)
    lon_back = jnp.einsum(
        "ie,mejl->mijl",
        band_matrix(kernel_lon, lon_tile, True),
        lat_back,
        preferred_element_type=jnp.float32,
    )
    new_controls = controls - descent * (controls + lon_back)
    return (new_controls, residual[None, None, None])


def solution(mesh):
    placed = (
        P("mem", "lon", "lat", None),
        P("mem", "lon", "lat", None),
        P(),
        P(),
        P("lon", "lat", "mem", None),
        P("lon", "lat", "mem"),
        P("lon", "lat", "mem", None),
        P("lon", "lat", "mem", None, None),
    )
    return jax.shard_map(
        shards,
        mesh=mesh,
        in_specs=placed,
        out_specs=(P("mem", "lon", "lat", None), P("lon", "lat", "mem", None, None)),
        check_vma=False,
    )
```

profile of v0, /device:TPU:1, one launch (start us, length us, event | category | flops | bytes accessed | tf_op | source)
XLA Modules:
  0.0 381.4 jit_solution(866354413344609248)
XLA Ops:
  7.2 0.0 copy-start.4
  7.2 0.0 copy-start.3
  7.2 0.0 copy-start.5
  7.2 0.0 all-reduce.3.cloned.1.call-start
  7.2 1.4 convert_element_type.70
  8.6 4.8 %collective-permute-start = (bf16[4,8,24,128]{3,2,1,0:T(8,128)(2,1)S(1)}, bf16[4,8,24,128]{3,2,1,0:T(8,128)(2,1)S(1)}, u32[]{:S(2)}, u32[]{:S(2)}) collective-permute-start(bf16[4,8,24,128]{3,2,1,0:T(8,128)(2,1)S(1)} %get-tuple-element.16), channel_id=1, source_target_pairs={{0,64},{64,128},{128,192},{192,256},{256,320},{320,384},{384,448},... | collective-permute-start | bytes 589832 | tf_op jit(solution)/shard_map/ppermute | solution.py:16
  13.5 15.9 %collective-permute-start.1 = (bf16[4,8,24,128]{3,2,1,0:T(8,128)(2,1)S(1)}, bf16[4,8,24,128]{3,2,1,0:T(8,128)(2,1)S(1)}, u32[]{:S(2)}, u32[]{:S(2)}) collective-permute-start(bf16[4,8,24,128]{3,2,1,0:T(8,128)(2,1)S(1)} %get-tuple-element.17), channel_id=1, source_target_pairs={{64,0},{128,64},{192,128},{256,192},{320,256},{384,320},{448,384},... | collective-permute-start | bytes 589832 | tf_op jit(solution)/shard_map/ppermute | solution.py:17
  29.4 0.0 copy-done.4
  29.4 0.0 copy-done.3
  29.4 0.1 rev.6
  29.5 0.1 rev.7
  30.3 0.2 select_reduce_fusion
  30.4 0.0 copy-done.5
  30.4 1.6 collective-permute-done
  32.0 0.9 collective-permute-done.1
  32.9 0.1 pad_maximum_fusion.5
  33.0 6.1 %collective-permute-start.2 = (bf16[4,40,8,128]{3,2,1,0:T(8,128)(2,1)S(1)}, bf16[4,40,8,128]{3,2,1,0:T(8,128)(2,1)S(1)}, u32[]{:S(2)}, u32[]{:S(2)}) collective-permute-start(bf16[4,40,8,128]{3,2,1,0:T(8,128)(2,1)S(1)} %get-tuple-element.12), channel_id=1, source_target_pairs={{0,16},{16,32},{32,48},{48,0},{1,17},{17,33},{33,49},{49,1},{2,18}... | collective-permute-start | bytes 983048 | tf_op jit(solution)/shard_map/ppermute | solution.py:16
  39.1 1.9 collective-permute-start.3
  41.1 2.8 collective-permute-done.2
  43.9 5.1 %collective-permute-done.3 = bf16[4,40,8,128]{3,2,1,0:T(8,128)(2,1)S(1)} collective-permute-done((bf16[4,40,8,128]{3,2,1,0:T(8,128)(2,1)S(1)}, bf16[4,40,8,128]{3,2,1,0:T(8,128)(2,1)S(1)}, u32[]{:S(2)}, u32[]{:S(2)}) %collective-permute-start.3) | collective-permute-done | bytes 327712 | tf_op jit(solution)/shard_map/ppermute | solution.py:17
  49.0 0.4 maximum_select_fusion
  49.4 0.0 copy-start.1
  49.4 0.4 fusion.9
  49.8 0.0 copy-start.6
  49.8 0.0 copy-start.2
  49.8 0.6 copy-done.1
  50.5 1.0 fusion.15
  51.5 0.0 all-reduce.3.cloned.1.call-update
  51.5 0.0 all-reduce.5.cloned.1.call-start
  51.6 0.0 copy-done.6
  51.6 132.7 %all-reduce.3.cloned.1.call-done = f32[576,128]{1,0:T(8,128)} async-done(((f32[576,128]{1,0:T(8,128)}), f32[576,128]{1,0:T(8,128)}) %all-reduce.3.cloned.1.call-update) | async-done | bytes 294928 | tf_op jit(solution)/shard_map/psum | solution.py:65
  184.3 1.5 gather_fusion
  185.8 0.0 copy-done.2
  185.8 0.8 scatter_custom_fusion
  186.6 0.7 convert_element_type.79
  187.3 0.0 all-reduce.5.cloned.1.call-update
  187.3 145.0 %all-reduce.5.cloned.1.call-done = bf16[24,24,128]{2,1,0:T(8,128)(2,1)} async-done(((bf16[24,24,128]{2,1,0:T(8,128)(2,1)}), bf16[24,24,128]{2,1,0:T(8,128)(2,1)}) %all-reduce.5.cloned.1.call-update) | async-done | bytes 147472 | tf_op jit(solution)/shard_map/psum | solution.py:74
  332.3 0.9 mul.92
  333.3 0.1 fusion.16
  333.4 3.3 collective-permute-start.4
  336.7 5.7 %collective-permute-start.5 = (bf16[4,8,24,128]{3,2,1,0:T(8,128)(2,1)S(1)}, bf16[4,8,24,128]{3,2,1,0:T(8,128)(2,1)S(1)}, u32[]{:S(2)}, u32[]{:S(2)}) collective-permute-start(bf16[4,8,24,128]{3,2,1,0:T(8,128)(2,1)S(1)} %get-tuple-element.15), channel_id=1, source_target_pairs={{64,0},{128,64},{192,128},{256,192},{320,256},{384,320},{448,384},... | collective-permute-start | bytes 589832 | tf_op jit(solution)/shard_map/ppermute | solution.py:17
  342.4 1.1 collective-permute-done.4
  343.5 1.5 collective-permute-done.5
  345.0 0.1 pad_maximum_fusion.2
  345.1 16.7 %collective-permute-start.6 = (bf16[4,40,8,128]{3,2,1,0:T(8,128)(2,1)S(1)}, bf16[4,40,8,128]{3,2,1,0:T(8,128)(2,1)S(1)}, u32[]{:S(2)}, u32[]{:S(2)}) collective-permute-start(bf16[4,40,8,128]{3,2,1,0:T(8,128)(2,1)S(1)} %get-tuple-element.10), channel_id=1, source_target_pairs={{0,16},{16,32},{32,48},{48,0},{1,17},{17,33},{33,49},{49,1},{2,18}... | collective-permute-start | bytes 983048 | tf_op jit(solution)/shard_map/ppermute | solution.py:16
  361.8 1.9 collective-permute-start.7
  363.7 0.7 fusion.25
  364.4 2.1 collective-permute-done.6
  366.5 5.2 %collective-permute-done.7 = bf16[4,40,8,128]{3,2,1,0:T(8,128)(2,1)S(1)} collective-permute-done((bf16[4,40,8,128]{3,2,1,0:T(8,128)(2,1)S(1)}, bf16[4,40,8,128]{3,2,1,0:T(8,128)(2,1)S(1)}, u32[]{:S(2)}, u32[]{:S(2)}) %collective-permute-start.7) | collective-permute-done | bytes 327712 | tf_op jit(solution)/shard_map/ppermute | solution.py:17
  371.7 0.0 copy-start
  371.7 0.5 fusion
  372.2 0.8 copy-done
  373.0 0.4 fusion.14
  373.4 1.2 copy.15
  (11 shorter events, 0.1 us)
Async XLA Ops:
  7.2 22.2 %copy-start.4 = (f32[17]{0:T(128)S(1)}, f32[17]{0:T(128)}, u32[]{:S(2)}) copy-start(f32[17]{0:T(128)} %param.10) | copy-start | bytes 208
  7.2 22.2 %copy-start.3 = (f32[17]{0:T(128)S(1)}, f32[17]{0:T(128)}, u32[]{:S(2)}) copy-start(f32[17]{0:T(128)} %param.11) | copy-start | bytes 208
  7.2 23.2 %copy-start.5 = (s32[1,1,1,16]{3,2,1,0:T(1,128)S(1)}, s32[1,1,1,16]{3,2,1,0:T(1,128)}, u32[]{:S(2)}) copy-start(s32[1,1,1,16]{3,2,1,0:T(1,128)} %param.12) | copy-start | bytes 196
  7.2 177.1 %all-reduce.3.cloned.1.call-start = ((), (), s32[]{:S(2)}) async-start(), calls=%async_computation | async-start | bytes 589824 | tf_op jit(solution)/shard_map/psum | solution.py:65
  8.6 23.4 %collective-permute-start = (bf16[4,8,24,128]{3,2,1,0:T(8,128)(2,1)S(1)}, bf16[4,8,24,128]{3,2,1,0:T(8,128)(2,1)S(1)}, u32[]{:S(2)}, u32[]{:S(2)}) collective-permute-start(bf16[4,8,24,128]{3,2,1,0:T(8,128)(2,1)S(1)} %get-tuple-element.16), channel_id=1, source_target_pairs={{0,64},{64,128},{128,192},{192,256},{256,320},{320,384},{384,448},... | collective-permute-start | bytes 589832 | tf_op jit(solution)/shard_map/ppermute | solution.py:16
  13.5 19.4 %collective-permute-start.1 = (bf16[4,8,24,128]{3,2,1,0:T(8,128)(2,1)S(1)}, bf16[4,8,24,128]{3,2,1,0:T(8,128)(2,1)S(1)}, u32[]{:S(2)}, u32[]{:S(2)}) collective-permute-start(bf16[4,8,24,128]{3,2,1,0:T(8,128)(2,1)S(1)} %get-tuple-element.17), channel_id=1, source_target_pairs={{64,0},{128,64},{192,128},{256,192},{320,256},{384,320},{448,384},... | collective-permute-start | bytes 589832 | tf_op jit(solution)/shard_map/ppermute | solution.py:17
  33.0 10.9 %collective-permute-start.2 = (bf16[4,40,8,128]{3,2,1,0:T(8,128)(2,1)S(1)}, bf16[4,40,8,128]{3,2,1,0:T(8,128)(2,1)S(1)}, u32[]{:S(2)}, u32[]{:S(2)}) collective-permute-start(bf16[4,40,8,128]{3,2,1,0:T(8,128)(2,1)S(1)} %get-tuple-element.12), channel_id=1, source_target_pairs={{0,16},{16,32},{32,48},{48,0},{1,17},{17,33},{33,49},{49,1},{2,18}... | collective-permute-start | bytes 983048 | tf_op jit(solution)/shard_map/ppermute | solution.py:16
  39.1 9.9 %collective-permute-start.3 = (bf16[4,40,8,128]{3,2,1,0:T(8,128)(2,1)S(1)}, bf16[4,40,8,128]{3,2,1,0:T(8,128)(2,1)S(1)}, u32[]{:S(2)}, u32[]{:S(2)}) collective-permute-start(bf16[4,40,8,128]{3,2,1,0:T(8,128)(2,1)S(1)} %get-tuple-element.13), channel_id=1, source_target_pairs={{16,0},{32,16},{48,32},{0,48},{17,1},{33,17},{49,33},{1,49},{18,2}... | collective-permute-start | bytes 983048 | tf_op jit(solution)/shard_map/ppermute | solution.py:17
  49.4 1.1 copy-start.1
  49.8 1.8 copy-start.6
  49.8 136.0 %copy-start.2 = (f32[1,1,1,16,128]{4,3,2,1,0:T(8,128)S(1)}, f32[1,1,1,16,128]{4,3,2,1,0:T(8,128)}, u32[]{:S(2)}) copy-start(f32[1,1,1,16,128]{4,3,2,1,0:T(8,128)} %param.15) | copy-start | bytes 24580
  51.5 280.8 %all-reduce.5.cloned.1.call-start = ((), (), s32[]{:S(2)}) async-start(), calls=%async_computation.1 | async-start | bytes 294912 | tf_op jit(solution)/shard_map/psum | solution.py:74
  333.4 10.1 %collective-permute-start.4 = (bf16[4,8,24,128]{3,2,1,0:T(8,128)(2,1)S(1)}, bf16[4,8,24,128]{3,2,1,0:T(8,128)(2,1)S(1)}, u32[]{:S(2)}, u32[]{:S(2)}) collective-permute-start(bf16[4,8,24,128]{3,2,1,0:T(8,128)(2,1)S(1)} %get-tuple-element.14), channel_id=1, source_target_pairs={{0,64},{64,128},{128,192},{192,256},{256,320},{320,384},{384,448},... | collective-permute-start | bytes 589832 | tf_op jit(solution)/shard_map/ppermute | solution.py:16
  336.7 8.3 %collective-permute-start.5 = (bf16[4,8,24,128]{3,2,1,0:T(8,128)(2,1)S(1)}, bf16[4,8,24,128]{3,2,1,0:T(8,128)(2,1)S(1)}, u32[]{:S(2)}, u32[]{:S(2)}) collective-permute-start(bf16[4,8,24,128]{3,2,1,0:T(8,128)(2,1)S(1)} %get-tuple-element.15), channel_id=1, source_target_pairs={{64,0},{128,64},{192,128},{256,192},{320,256},{384,320},{448,384},... | collective-permute-start | bytes 589832 | tf_op jit(solution)/shard_map/ppermute | solution.py:17
  345.1 21.4 %collective-permute-start.6 = (bf16[4,40,8,128]{3,2,1,0:T(8,128)(2,1)S(1)}, bf16[4,40,8,128]{3,2,1,0:T(8,128)(2,1)S(1)}, u32[]{:S(2)}, u32[]{:S(2)}) collective-permute-start(bf16[4,40,8,128]{3,2,1,0:T(8,128)(2,1)S(1)} %get-tuple-element.10), channel_id=1, source_target_pairs={{0,16},{16,32},{32,48},{48,0},{1,17},{17,33},{33,49},{49,1},{2,18}... | collective-permute-start | bytes 983048 | tf_op jit(solution)/shard_map/ppermute | solution.py:16
  361.8 9.9 %collective-permute-start.7 = (bf16[4,40,8,128]{3,2,1,0:T(8,128)(2,1)S(1)}, bf16[4,40,8,128]{3,2,1,0:T(8,128)(2,1)S(1)}, u32[]{:S(2)}, u32[]{:S(2)}) collective-permute-start(bf16[4,40,8,128]{3,2,1,0:T(8,128)(2,1)S(1)} %get-tuple-element.11), channel_id=1, source_target_pairs={{16,0},{32,16},{48,32},{0,48},{17,1},{33,17},{49,33},{1,49},{18,2}... | collective-permute-start | bytes 983048 | tf_op jit(solution)/shard_map/ppermute | solution.py:17
  371.7 1.3 copy-start
Sparse Core Ops, SparseCore 0:
  51.6 132.6 all-reduce.2
  188.4 143.9 all-reduce.4
where the time goes:
time: 382 us; the launch traced here: 381 us
  waiting for transfers between devices  298 us (78%)
  starting transfers between devices  56.3 us (15%)
  between operations  15 us (4%)
  other arithmetic  5.38 us (1%)
  local copies, waits for them, and re-layouts  4.45 us (1%)
    psum x1, waiting for transfers between devices, shards(): adjoint = lax.psum(placed.astype(jnp.bfloat16), 'mem').astype(jnp.float32)  145 us
    psum x1, waiting for transfers between devices, shards(): increment = lax.psum(flat_part, 'mem')  133 us
    ppermute x4, starting transfers between devices, extended_2(): before = lax.ppermute(last, axis, up)  30.8 us
    ppermute x4, starting transfers between devices, extended_2(): after = lax.ppermute(initial, axis, down)  25.4 us
    ppermute x4, waiting for transfers between devices, extended_2(): after = lax.ppermute(initial, axis, down)  12.6 us
    ppermute x4, waiting for transfers between devices, extended_2(): before = lax.ppermute(last, axis, up)  7.64 us
  transfers between devices with their start and end apart: 10, of which 10 were waited for; matrix products, arithmetic and copies ran while one was open for 0% of the time, Pallas kernels for 0%

commit v1 on v0

v1 whole, which is shorter than its diff:
```python
import functools

import jax
import jax.numpy as jnp
from jax import lax
from jax.experimental import pallas as pl
from jax.experimental.pallas import tpu as pltpu
from jax.sharding import PartitionSpec as P

LEV = 128
TILE = 24
HALF = 8
TAPS = 17
SLOTS = 16
MEM = 4
WIDE = MEM * LEV
CELLS = TILE * TILE
SIDE = TILE * HALF
CORNER = HALF * HALF
descent = 0.5
OFF_Z = 0
OFF_L = 2 * SIDE
OFF_X = 4 * SIDE
OFF_C = 4 * SIDE + 4 * CORNER
EXT = OFF_C + CELLS + 64
PAD_C = CELLS + 64
REGIONS = (
    (-1, 0, OFF_Z, SIDE),
    (1, 0, OFF_Z + SIDE, SIDE),
    (0, -1, OFF_L, SIDE),
    (0, 1, OFF_L + SIDE, SIDE),
    (-1, -1, OFF_X, CORNER),
    (1, -1, OFF_X + CORNER, CORNER),
    (-1, 1, OFF_X + 2 * CORNER, CORNER),
    (1, 1, OFF_X + 3 * CORNER, CORNER),
)
GROUPS = ((0, 2, OFF_Z, 2 * SIDE), (2, 4, OFF_L, 2 * SIDE), (4, 8, OFF_X, 4 * CORNER))
MESH = pl.DeviceIdType.MESH
f32 = jnp.float32
bf16 = jnp.bfloat16


def iota(shape, dim):
    return lax.broadcasted_iota(jnp.int32, shape, dim)


def by_tile(q):
    i = (q * 2731) >> 16
    return i, q - TILE * i


def column_coords():
    lon, lat = [], []
    def add(i, j):
        lon.append(i)
        lat.append(j)
    for base in (0, HALF + TILE):
        i, j = by_tile(iota((1, SIDE), 1))
        add(i + base, j + HALF)
    for base in (0, HALF + TILE):
        q = iota((1, SIDE), 1)
        add((q >> 3) + HALF, (q & 7) + base)
    for base_lat in (0, HALF + TILE):
        for base_lon in (0, HALF + TILE):
            q = iota((1, CORNER), 1)
            add((q >> 3) + base_lon, (q & 7) + base_lat)
    i, j = by_tile(iota((1, PAD_C), 1))
    ok = iota((1, PAD_C), 1) < CELLS
    add(jnp.where(ok, i + HALF, -1), jnp.where(ok, j + HALF, -1))
    return jnp.concatenate(lon, axis=1), jnp.concatenate(lat, axis=1)


def dot(a, b):
    return jnp.dot(a, b, preferred_element_type=f32)


def piece(dz, dl, field):
    i0, ni = {-1: (TILE - HALF, HALF), 1: (0, HALF), 0: (0, TILE)}[dz]
    j0 = {-1: TILE - HALF, 1: 0}[dl]
    part = field[i0:i0 + ni, j0:j0 + HALF, :]
    return part.reshape(ni * HALF, part.shape[2])


def kernel(sizes, ctrl_hbm, ens_hbm, tlon, tlat, cols, count, qual, vals, lb_ref, res_ref,
           ctrl, xall, eall, aall, xstage, estage, azs, astage, colall, gsend, grecv, rall, w2, k2, st, tabs, ensobs, acc,
           load_sem, rim_send, rim_recv, mem_send, mem_recv):
    n_lon, n_lat, n_mem = sizes
    z = lax.axis_index("lon")
    l = lax.axis_index("lat")
    me = lax.axis_index("mem")

    loads = [pltpu.make_async_copy(ctrl_hbm.at[m], ctrl.at[:, m * LEV:(m + 1) * LEV], load_sem.at[m]) for m in range(MEM)]
    loads_e = [
        pltpu.make_async_copy(ens_hbm.at[m], eall.at[OFF_C:OFF_C + CELLS, m * LEV:(m + 1) * LEV], load_sem.at[MEM + m])
        for m in range(MEM)
    ]
    for c in loads + loads_e:
        c.start()

    def lon_of(dz):
        return lax.rem(z + dz + n_lon, n_lon)

    def has(dl):
        if dl == 0:
            return None
        return (l + dl >= 0) & (l + dl < n_lat)

    def guarded(cond, f):
        if cond is None:
            f()
        else:
            pl.when(cond)(f)

    barrier = pltpu.get_barrier_semaphore()
    for dz, dl, _, _ in REGIONS:
        def greet(dz=dz, dl=dl):
            pl.semaphore_signal(barrier, inc=1, device_id={"lon": lon_of(dz), "lat": l + dl}, device_id_type=MESH)
        guarded(has(dl), greet)

    def greet_mem(t, _):
        pl.semaphore_signal(barrier, inc=1, device_id={"mem": lax.rem(me + t, n_mem)}, device_id_type=MESH)
        return 0
    lax.fori_loop(1, n_mem, greet_mem, 0)

    slot = iota((SLOTS, LEV), 0)
    col = jnp.zeros((SLOTS, LEV), jnp.int32)
    quality = jnp.zeros((SLOTS, LEV), f32)
    for s in range(SLOTS):
        col = jnp.where(slot == s, cols[s], col)
        quality = jnp.where(slot == s, qual[s].astype(f32), quality)
    weights = jnp.where(slot < count[0], 0.5 * quality, 0.0)
    mine = pl.ds(pl.multiple_of(me * SLOTS, SLOTS), SLOTS)
    colall[mine, :] = col

    for c in loads:
        c.wait()
    field = ctrl[...]
    xall[OFF_C:OFF_C + CELLS, :] = field.astype(bf16)
    xall[OFF_C + CELLS:EXT, :] = jnp.zeros((64, WIDE), bf16)
    eall[OFF_C + CELLS:EXT, :] = jnp.zeros((64, WIDE), bf16)
    field = field.reshape(TILE, TILE, WIDE)
    for dz, dl, row, rows in REGIONS[2:]:
        xstage[row - OFF_L:row - OFF_L + rows, :] = piece(dz, dl, field).astype(bf16)

    for dl, row, xrow in ((-1, OFF_L, OFF_X), (1, OFF_L + SIDE, OFF_X + 2 * CORNER)):
        @pl.when(jnp.logical_not(has(dl)))
        def _(row=row, xrow=xrow):
            for ref in (xall, eall):
                ref[row:row + SIDE, :] = jnp.zeros((SIDE, WIDE), bf16)
                ref[xrow:xrow + 2 * CORNER, :] = jnp.zeros((2 * CORNER, WIDE), bf16)
            aall[row:row + SIDE, :] = jnp.zeros((SIDE, LEV), bf16)
            aall[xrow:xrow + 2 * CORNER, :] = jnp.zeros((2 * CORNER, LEV), bf16)

    both = jnp.where((l > 0) & (l < n_lat - 1), 8, 5)
    pl.semaphore_wait(barrier, both + n_mem - 1)

    def rim_copy(kind, d, own, own_row, stage, dst):
        dz, dl, row, rows = REGIONS[d]
        if dl == 0:
            first = own_row + (CELLS - SIDE if dz == -1 else 0)
            src = own.at[first:first + rows, :]
        else:
            src = stage.at[row - OFF_L:row - OFF_L + rows, :]
        return pltpu.make_async_remote_copy(
            src_ref=src, dst_ref=dst.at[row:row + rows, :],
            send_sem=rim_send.at[kind, d], recv_sem=rim_recv.at[kind, d],
            device_id={"lon": lon_of(-dz), "lat": l - dl}, device_id_type=MESH)

    def start_rims(copies):
        for d, c in enumerate(copies):
            guarded(has(-REGIONS[d][1]), c.start)

    def recv_rims(copies, lo, hi):
        for d in range(lo, hi):
            guarded(has(REGIONS[d][1]), copies[d].wait_recv)

    def sent_rims(copies):
        for d, c in enumerate(copies):
            guarded(has(-REGIONS[d][1]), c.wait_send)

    def rows_of(index):
        return pl.ds(pl.multiple_of(index * SLOTS, SLOTS), SLOTS)

    def mem_copy(kind, t, src_of, dst):
        peer = lax.rem(me + t, n_mem)
        return pltpu.make_async_remote_copy(
            src_ref=src_of(peer), dst_ref=dst.at[mine, :],
            send_sem=mem_send.at[kind, t], recv_sem=mem_recv.at[kind, t],
            device_id={"mem": peer}, device_id_type=MESH)

    def mem_loop(kind, src_of, dst, what):
        def step(t, _):
            getattr(mem_copy(kind, t, src_of, dst), what)()
            return 0
        lax.fori_loop(1, n_mem, step, 0)

    col_of = lambda peer: colall.at[mine, :]
    g_of = lambda peer: gsend.at[rows_of(peer), :]
    r_of = lambda peer: rall.at[mine, :]

    xrims = [rim_copy(0, d, xall, OFF_C, xstage, xall) for d in range(8)]
    erims = [rim_copy(1, d, eall, OFF_C, estage, eall) for d in range(8)]
    arims = [rim_copy(2, d, azs, 0, astage, aall) for d in range(8)]

    mem_loop(0, col_of, colall, "start")
    start_rims(xrims)

    for c in loads_e:
        c.wait()
    field = eall[OFF_C:OFF_C + CELLS, :].astype(f32).reshape(TILE, TILE, WIDE)
    for dz, dl, row, rows in REGIONS[2:]:
        estage[row - OFF_L:row - OFF_L + rows, :] = piece(dz, dl, field).astype(bf16)
    start_rims(erims)

    shift = iota((32, 48), 1) - iota((32, 48), 0)
    lon_q, lat_q = column_coords()
    for index, (tap, coord) in enumerate(((tlon, lon_q), (tlat, lat_q))):
        here = jnp.where(iota((48, EXT), 0) == jnp.broadcast_to(coord, (48, EXT)), 1.0, 0.0).astype(bf16)
        ahead = jnp.zeros((32, 48), f32)
        back = jnp.zeros((32, 48), f32)
        for k in range(TAPS):
            ahead = jnp.where(shift == k, tap[k], ahead)
            back = jnp.where(shift == k, tap[TAPS - 1 - k], back)
        if index == 1:
            back = -descent * back
        tabs[index] = dot(ahead.astype(bf16), here).astype(bf16)
        tabs[2 + index] = dot(back.astype(bf16), here).astype(bf16)

    mem_loop(0, col_of, colall, "wait_recv")
    total = n_mem * SLOTS
    column = colall[...]
    own_i, own_j = by_tile(column)
    lane = iota((total, LEV), 1)
    pick_i = jnp.where(lane == own_i, 1.0, 0.0).astype(bf16)[:, :32]
    pick_j = jnp.where(lane == own_j, 1.0, 0.0).astype(bf16)[:, :32]
    for q in range(0, EXT, 128):
        part = dot(pick_i, tabs[0, :, q:q + 128]) * dot(pick_j, tabs[1, :, q:q + 128])
        w2[:, q:q + 128] = part.astype(bf16)
    select = jnp.concatenate(
        [jnp.where(lane + q == column, 1.0, 0.0).astype(bf16) for q in range(0, PAD_C, 128)], axis=1)
    ensobs[...] = dot(select, eall[OFF_C:EXT, :])
    column_t = jnp.transpose(column.astype(f32))[0:1, :]
    cell = iota((CELLS, total), 0).astype(f32)
    st[...] = jnp.where(cell == jnp.broadcast_to(column_t, (CELLS, total)), 1.0, 0.0).astype(bf16)

    acc[...] = dot(w2[:, OFF_C:EXT], xall[OFF_C:EXT, :])
    for lo, hi, row, rows in GROUPS:
        recv_rims(xrims, lo, hi)
        acc[...] += dot(w2[:, row:row + rows], xall[row:row + rows, :])
    product = acc[...] * ensobs[...]
    part = product[:, 0:LEV]
    for m in range(1, MEM):
        part = part + product[:, m * LEV:(m + 1) * LEV]
    gsend[...] = part.astype(bf16)
    mem_loop(1, g_of, grecv, "start")
    grecv[mine, :] = gsend[mine, :]

    def build(b, _):
        rows = pl.ds(pl.multiple_of(b * 64, 64), 64)
        r = iota((64, 32), 0) + b * 64
        i, j = by_tile(r)
        lanes = iota((64, 32), 1)
        at_i = jnp.where(lanes == i, 1.0, 0.0).astype(bf16)
        at_j = jnp.where(lanes == j, 1.0, 0.0).astype(bf16)
        for q in range(0, EXT, 128):
            part = dot(at_i, tabs[2, :, q:q + 128]) * dot(at_j, tabs[3, :, q:q + 128])
            k2[rows, q:q + 128] = part.astype(bf16)
        return 0
    lax.fori_loop(0, CELLS // 64, build, 0)

    mem_loop(1, g_of, grecv, "wait_recv")
    observed = jnp.zeros((SLOTS, LEV), f32)
    for o in range(n_mem):
        observed = observed + grecv[o * SLOTS:(o + 1) * SLOTS, :].astype(f32)
    residual = weights * (observed - vals[...])
    res_ref[...] = residual
    rall[mine, :] = residual.astype(bf16)
    mem_loop(2, r_of, rall, "start")
    recv_rims(erims, 0, 8)
    mem_loop(2, r_of, rall, "wait_recv")

    adjoint = dot(st[...], rall[...])
    azs[...] = adjoint.astype(bf16)
    field = adjoint.reshape(TILE, TILE, LEV)
    for dz, dl, row, rows in REGIONS[2:]:
        astage[row - OFF_L:row - OFF_L + rows, :] = piece(dz, dl, field).astype(bf16)
    start_rims(arims)

    def backward(row, rows, adj):
        wide = jnp.concatenate([adj] * MEM, axis=1)
        weighted = (eall[row:row + rows, :].astype(f32) * wide).astype(bf16)
        return dot(k2[:, row:row + rows], weighted)

    zero = jnp.zeros((PAD_C - CELLS, LEV), f32)
    back = backward(OFF_C, PAD_C, jnp.concatenate([adjoint, zero], axis=0))
    for m in range(MEM):
        lb_ref[m] = back[:, m * LEV:(m + 1) * LEV].reshape(TILE, TILE, LEV)
    for lo, hi, row, rows in GROUPS:
        recv_rims(arims, lo, hi)
        back = backward(row, rows, aall[row:row + rows, :].astype(f32))
        for m in range(MEM):
            lb_ref[m] += back[:, m * LEV:(m + 1) * LEV].reshape(TILE, TILE, LEV)

    for copies in (xrims, erims, arims):
        sent_rims(copies)
    mem_loop(0, col_of, colall, "wait_send")
    mem_loop(1, g_of, grecv, "wait_send")
    mem_loop(2, r_of, rall, "wait_send")


def shards(sizes, controls, ensemble, taps_lon, taps_lat, obs_columns, obs_count, obs_quality, obs_values):
    total = sizes[2] * SLOTS
    smem = pl.BlockSpec(memory_space=pltpu.SMEM)
    vmem = pl.BlockSpec(memory_space=pltpu.VMEM)
    hbm = pl.BlockSpec(memory_space=pl.ANY)
    step, residual = pl.pallas_call(
        functools.partial(kernel, sizes),
        out_shape=(jax.ShapeDtypeStruct((MEM, TILE, TILE, LEV), f32), jax.ShapeDtypeStruct((SLOTS, LEV), f32)),
        in_specs=[hbm, hbm, smem, smem, smem, smem, smem, vmem],
        out_specs=(vmem, vmem),
        scratch_shapes=[
            pltpu.VMEM((CELLS, WIDE), f32),
            pltpu.VMEM((EXT, WIDE), bf16),
            pltpu.VMEM((EXT, WIDE), bf16),
            pltpu.VMEM((EXT, LEV), bf16),
            pltpu.VMEM((OFF_C - OFF_L, WIDE), bf16),
            pltpu.VMEM((OFF_C - OFF_L, WIDE), bf16),
            pltpu.VMEM((CELLS, LEV), bf16),
            pltpu.VMEM((OFF_C - OFF_L, LEV), bf16),
            pltpu.VMEM((total, LEV), jnp.int32),
            pltpu.VMEM((total, LEV), bf16),
            pltpu.VMEM((total, LEV), bf16),
            pltpu.VMEM((total, LEV), bf16),
            pltpu.VMEM((total, EXT), bf16),
            pltpu.VMEM((CELLS, EXT), bf16),
            pltpu.VMEM((CELLS, total), bf16),
            pltpu.VMEM((4, 32, EXT), bf16),
            pltpu.VMEM((total, WIDE), f32),
            pltpu.VMEM((total, WIDE), f32),
            pltpu.SemaphoreType.DMA((2 * MEM,)),
            pltpu.SemaphoreType.DMA((3, 8)),
            pltpu.SemaphoreType.DMA((3, 8)),
            pltpu.SemaphoreType.DMA((3, sizes[2])),
            pltpu.SemaphoreType.DMA((3, sizes[2])),
        ],
        compiler_params=pltpu.CompilerParams(collective_id=0, has_side_effects=True, vmem_limit_bytes=63 * 1024 * 1024),
        name="step",
    )(
        controls.reshape(MEM, CELLS, LEV),
        ensemble.reshape(MEM, CELLS, LEV),
        taps_lon,
        taps_lat,
        obs_columns.reshape(SLOTS),
        obs_count.reshape(1),
        obs_quality.reshape(SLOTS),
        obs_values.reshape(SLOTS, LEV),
    )
    new_controls = (1.0 - descent) * controls + step
    return new_controls, residual.reshape(obs_values.shape)


def solution(mesh):
    sizes = (mesh.shape["lon"], mesh.shape["lat"], mesh.shape["mem"])
    placed = (
        P("mem", "lon", "lat", None),
        P("mem", "lon", "lat", None),
        P(),
        P(),
        P("lon", "lat", "mem", None),
        P("lon", "lat", "mem"),
        P("lon", "lat", "mem", None),
        P("lon", "lat", "mem", None, None),
    )
    return jax.shard_map(
        functools.partial(shards, sizes),
        mesh=mesh,
        in_specs=placed,
        out_specs=(P("mem", "lon", "lat", None), P("lon", "lat", "mem", None, None)),
        check_vma=False,
    )
```

time: 382 us -> 56.8 us (0.15)
  waiting for transfers between devices: 298 us -> 0 us
  starting transfers between devices: 56.3 us -> 0 us
  Pallas kernels: 0 us -> 51.9 us
  between operations: 15 us -> 1.29 us
  local copies, waits for them, and re-layouts: 4.45 us -> 0.6 us
    psum x2 -> x0, waiting for transfers between devices: 278 us -> none  [the longest x1 145 us: shards(): adjoint = lax.psum(placed.astype(jnp.bfloat16), 'mem').astype(jnp.float32)]
    ppermute x8 -> x0, starting transfers between devices: 56.2 us -> none  [the longest x4 30.8 us: extended_2(): before = lax.ppermute(last, axis, up)]
    pallas_call x0 -> x1, Pallas kernels: none -> 51.9 us  [shards(): pl.pallas_call(functools.partial(kernel, sizes), out_shape=(jax.ShapeDtyp...]
    ppermute x8 -> x0, waiting for transfers between devices: 20.3 us -> none  [the longest x4 12.6 us: extended_2(): after = lax.ppermute(initial, axis, down)]
  transfers between devices with their start and end apart: 10 -> 0, of which waited for: 10 -> 0; matrix products, arithmetic and copies ran while one was open for 0% -> 0% of each run, Pallas kernels for 0% -> 0%
where the time goes in v1:
time: 56.8 us; the launch traced here: 56.6 us
  Pallas kernels  51.9 us (91%)
  other arithmetic  2.76 us (5%)
  between operations  1.29 us (2%)
  local copies, waits for them, and re-layouts  0.6 us (1%)
    pallas_call x1, Pallas kernels, shards(): pl.pallas_call(functools.partial(kernel, sizes), out_shape=(jax.ShapeDtyp...  51.9 us
    add x1, other arithmetic, shards(): new_controls = (1.0 - descent) * controls + step  2.76 us

profile of v1, /device:TPU:1, one launch (start us, length us, event | category | flops | bytes accessed | tf_op | source)
XLA Modules:
  0.0 56.6 jit_solution(2873447407204917330)
XLA Ops:
  1.3 51.9 %step.1 = (f32[4,24,24,128]{3,2,1,0:T(8,128)}, f32[16,128]{1,0:T(8,128)}) custom-call(f32[4,576,128]{2,1,0:T(8,128)} %bitcast.8, bf16[4,576,128]{2,1,0:T(8,128)(2,1)} %bitcast.9, f32[17]{0:T(128)} %tlon.1, f32[17]{0:T(128)} %tlat.1, s32[16]{0:T(128)} %bitcast.12, s32[1]{0:T(128)} %bitcast.7.count, s32[16]{0:T(128)} %bitcast.13, f32[16,128]{1,0:T(8,128)} %bitcast.10), custom_call_target="tpu_custom_call" | custom-call | tf_op jit(solution)/shard_map/step/pallas_call | solution.py:316
  53.2 0.0 copy-start
  53.2 2.8 %multiply_add_fusion = f32[4,24,24,128]{3,2,1,0:T(8,128)} fusion(f32[4,24,24,128]{3,2,1,0:T(8,128)} %get-tuple-element.4, f32[4,24,24,128]{3,2,1,0:T(8,128)} %param.8), kind=kLoop, calls=%fused_computation | loop fusion | flops 589824 | bytes 3538944 | tf_op jit(solution)/shard_map/add | solution.py:358
  56.0 0.0 copy-done
  56.0 0.6 %copy.12 = f32[1,1,1,16,128]{4,3,2,1,0:T(8,128)} copy(f32[1,1,1,16,128]{4,3,2,1,0:T(8,128)S(1)} %bitcast.11) | data formatting | bytes 16384
Async XLA Ops:
  53.2 2.8 %copy-start = (f32[16,128]{1,0:T(8,128)S(1)}, f32[16,128]{1,0:T(8,128)}, u32[]{:S(2)}) copy-start(f32[16,128]{1,0:T(8,128)} %get-tuple-element.5) | copy-start | bytes 24580

commit v2 on v1

v2 whole, which is shorter than its diff:
```python
import functools

import jax
import jax.numpy as jnp
from jax import lax
from jax.experimental import pallas as pl
from jax.experimental.pallas import tpu as pltpu
from jax.sharding import PartitionSpec as P

LEV = 128
TILE = 24
HALF = 8
TAPS = 17
SLOTS = 16
MEM = 4
WIDE = MEM * LEV
CELLS = TILE * TILE
SIDE = TILE * HALF
CORNER = HALF * HALF
descent = 0.5
OFF_Z = 0
OFF_L = 2 * SIDE
OFF_X = 4 * SIDE
OFF_C = 4 * SIDE + 4 * CORNER
EXT = OFF_C + CELLS + 64
PAD_C = CELLS + 64
REGIONS = (
    (-1, 0, OFF_Z, SIDE),
    (1, 0, OFF_Z + SIDE, SIDE),
    (0, -1, OFF_L, SIDE),
    (0, 1, OFF_L + SIDE, SIDE),
    (-1, -1, OFF_X, CORNER),
    (1, -1, OFF_X + CORNER, CORNER),
    (-1, 1, OFF_X + 2 * CORNER, CORNER),
    (1, 1, OFF_X + 3 * CORNER, CORNER),
)
GROUPS = ((0, 2, OFF_Z, 2 * SIDE), (2, 4, OFF_L, 2 * SIDE), (4, 8, OFF_X, 4 * CORNER))
MESH = pl.DeviceIdType.MESH
f32 = jnp.float32
bf16 = jnp.bfloat16


def iota(shape, dim):
    return lax.broadcasted_iota(jnp.int32, shape, dim)


def by_tile(q):
    i = (q * 2731) >> 16
    return i, q - TILE * i


def column_coords():
    lon, lat = [], []
    def add(i, j):
        lon.append(i)
        lat.append(j)
    for base in (0, HALF + TILE):
        i, j = by_tile(iota((1, SIDE), 1))
        add(i + base, j + HALF)
    for base in (0, HALF + TILE):
        q = iota((1, SIDE), 1)
        add((q >> 3) + HALF, (q & 7) + base)
    for base_lat in (0, HALF + TILE):
        for base_lon in (0, HALF + TILE):
            q = iota((1, CORNER), 1)
            add((q >> 3) + base_lon, (q & 7) + base_lat)
    i, j = by_tile(iota((1, PAD_C), 1))
    ok = iota((1, PAD_C), 1) < CELLS
    add(jnp.where(ok, i + HALF, -1), jnp.where(ok, j + HALF, -1))
    return jnp.concatenate(lon, axis=1), jnp.concatenate(lat, axis=1)


def dot(a, b):
    return jnp.dot(a, b, preferred_element_type=f32)


def piece(dz, dl, field):
    i0, ni = {-1: (TILE - HALF, HALF), 1: (0, HALF), 0: (0, TILE)}[dz]
    j0 = {-1: TILE - HALF, 1: 0}[dl]
    part = field[i0:i0 + ni, j0:j0 + HALF, :]
    return part.reshape(ni * HALF, part.shape[2])


def region_coords(d, n):
    dz, dl, _, _ = REGIONS[d]
    start = {-1: 0, 0: HALF, 1: HALF + TILE}
    q = iota((1, n), 1)
    i, j = by_tile(q) if dl == 0 else (q >> 3, q & 7)
    return i + start[dz], j + start[dl]


def block_of(ref, m, d):
    dz, dl, _, _ = REGIONS[d]
    part = {-1: slice(0, HALF), 0: slice(0, TILE), 1: slice(TILE - HALF, TILE)}
    return ref.at[m, part[dz], part[dl], :]


def one_hot(index, n):
    return jnp.where(iota((index.shape[0], n), 1) == index, 1.0, 0.0).astype(bf16)


def kernel(sizes, ctrl_hbm, ens_hbm, tlon_hbm, tlat_hbm, cols_hbm, count, qual_hbm, vals_hbm, out_ref, res_ref,
           ctrl, xall, eall, aall, xstage, estage, azs, astage, colall, gsend, grecv, rall, w2, k2c, k2z, k2l, k2x, st, tabs,
           back_tabs, ensobs, acc, tlon, tlat, cols, qual, vals,
           load_sem, small_sem, rim_send, rim_recv, mem_send, mem_recv):
    n_lon, n_lat, n_mem = sizes
    n_y = n_mem // 2
    z = lax.axis_index("lon")
    l = lax.axis_index("lat")
    me = lax.axis_index("mem")
    my_x, my_y = me // n_y, lax.rem(me, n_y)

    def lon_of(dz):
        return lax.rem(z + dz + n_lon, n_lon)

    def has(dl):
        if dl == 0:
            return None
        return (l + dl >= 0) & (l + dl < n_lat)

    def guarded(cond, f):
        if cond is None:
            f()
        else:
            pl.when(cond)(f)

    steps = [(dx, dy) for dy in sorted(range(n_y), key=lambda y: -min(y, n_y - y)) for dx in (1, 0)]
    steps = [s for s in steps if s != (0, 0)]

    def peer_of(dx, dy):
        return lax.rem(my_x + dx, 2) * n_y + lax.rem(my_y + dy, n_y)

    barrier = pltpu.get_barrier_semaphore()
    for dx, dy in steps:
        pl.semaphore_signal(barrier, inc=1, device_id={"mem": peer_of(dx, dy)}, device_id_type=MESH)
    for dz, dl, _, _ in REGIONS:
        def greet(dz=dz, dl=dl):
            pl.semaphore_signal(barrier, inc=1, device_id={"lon": lon_of(dz), "lat": l + dl}, device_id_type=MESH)
        guarded(has(dl), greet)

    loads = [pltpu.make_async_copy(ctrl_hbm.at[m], ctrl.at[:, m * LEV:(m + 1) * LEV], load_sem.at[m]) for m in range(MEM)]
    loads_e = [
        pltpu.make_async_copy(ens_hbm.at[m], eall.at[OFF_C:OFF_C + CELLS, m * LEV:(m + 1) * LEV], load_sem.at[MEM + m])
        for m in range(MEM)
    ]
    pairs = ((cols_hbm, cols), (qual_hbm, qual), (tlon_hbm, tlon), (tlat_hbm, tlat), (vals_hbm, vals))
    small = [pltpu.make_async_copy(a, b, small_sem.at[k]) for k, (a, b) in enumerate(pairs)]
    for c in loads + small + loads_e:
        c.start()

    xall[OFF_C + CELLS:EXT, :] = jnp.zeros((64, WIDE), bf16)
    eall[OFF_C + CELLS:EXT, :] = jnp.zeros((64, WIDE), bf16)
    for dl, row, xrow in ((-1, OFF_L, OFF_X), (1, OFF_L + SIDE, OFF_X + 2 * CORNER)):
        @pl.when(jnp.logical_not(has(dl)))
        def _(row=row, xrow=xrow):
            for ref in (xall, eall):
                ref[row:row + SIDE, :] = jnp.zeros((SIDE, WIDE), bf16)
                ref[xrow:xrow + 2 * CORNER, :] = jnp.zeros((2 * CORNER, WIDE), bf16)
            aall[row:row + SIDE, :] = jnp.zeros((SIDE, LEV), bf16)
            aall[xrow:xrow + 2 * CORNER, :] = jnp.zeros((2 * CORNER, LEV), bf16)

    for c in small:
        c.wait()
    lane1 = iota((1, LEV), 1)
    col = jnp.zeros((1, LEV), jnp.int32)
    for s in range(SLOTS):
        col = jnp.where(lane1 == s, cols[0, 0, 0, s], col)
    colall[me] = col

    for c in loads:
        c.wait()
    field = ctrl[...]
    xall[OFF_C:OFF_C + CELLS, :] = field.astype(bf16)
    field = field.reshape(TILE, TILE, WIDE)
    for dz, dl, row, rows in REGIONS[2:]:
        xstage[row - OFF_L:row - OFF_L + rows, :] = piece(dz, dl, field).astype(bf16)

    both = jnp.where((l > 0) & (l < n_lat - 1), 8, 5)
    pl.semaphore_wait(barrier, both + n_mem - 1)

    def rim_copy(kind, d, own, own_row, stage, dst):
        dz, dl, row, rows = REGIONS[d]
        if dl == 0:
            first = own_row + (CELLS - SIDE if dz == -1 else 0)
            src = own.at[first:first + rows, :]
        else:
            src = stage.at[row - OFF_L:row - OFF_L + rows, :]
        return pltpu.make_async_remote_copy(
            src_ref=src, dst_ref=dst.at[row:row + rows, :],
            send_sem=rim_send.at[kind, d], recv_sem=rim_recv.at[kind, d],
            device_id={"lon": lon_of(-dz), "lat": l - dl}, device_id_type=MESH)

    def crosses(d):
        return lax.rem(l, 2) == (1 if REGIONS[d][1] == -1 else 0)

    def start_rims(copies):
        for d, c in enumerate(copies):
            guarded(has(-REGIONS[d][1]), c.start)

    def start_some(copies, which, across):
        for d in which:
            dl = REGIONS[d][1]
            if dl == 0:
                if not across:
                    copies[d].start()
            else:
                far = crosses(d)
                guarded(has(-dl) & (far if across else jnp.logical_not(far)), copies[d].start)

    def recv_rims(copies, lo, hi):
        for d in range(lo, hi):
            guarded(has(REGIONS[d][1]), copies[d].wait_recv)

    def sent_rims(copies):
        for d, c in enumerate(copies):
            guarded(has(-REGIONS[d][1]), c.wait_send)

    def rows_of(index):
        return pl.ds(pl.multiple_of(index * SLOTS, SLOTS), SLOTS)

    mine = rows_of(me)

    def mem_copies(kind, src_of, dst):
        made = []
        for t, (dx, dy) in enumerate(steps):
            peer = peer_of(dx, dy)
            made.append(pltpu.make_async_remote_copy(
                src_ref=src_of(peer), dst_ref=dst,
                send_sem=mem_send.at[kind, t], recv_sem=mem_recv.at[kind, t],
                device_id={"mem": peer}, device_id_type=MESH))
        return made

    xrims = [rim_copy(0, d, xall, OFF_C, xstage, xall) for d in range(8)]
    erims = [rim_copy(1, d, eall, OFF_C, estage, eall) for d in range(8)]
    arims = [rim_copy(2, d, azs, 0, astage, aall) for d in range(8)]
    ccopies = mem_copies(0, lambda peer: colall.at[me], colall.at[me])
    gcopies = mem_copies(1, lambda peer: gsend.at[rows_of(peer), :], grecv.at[mine, :])
    rcopies = mem_copies(2, lambda peer: rall.at[mine, :], rall.at[mine, :])

    for c in ccopies:
        c.start()
    start_rims(xrims)

    for c in loads_e:
        c.wait()
    field = eall[OFF_C:OFF_C + CELLS, :].astype(f32).reshape(TILE, TILE, WIDE)
    for dz, dl, row, rows in REGIONS[2:]:
        estage[row - OFF_L:row - OFF_L + rows, :] = piece(dz, dl, field).astype(bf16)
    start_some(erims, range(8), False)

    shift = iota((32, 48), 1) - iota((32, 48), 0)
    for index, (tap, coord) in enumerate(zip((tlon, tlat), column_coords())):
        here = jnp.where(iota((48, EXT), 0) == jnp.broadcast_to(coord, (48, EXT)), 1.0, 0.0).astype(bf16)
        ahead = jnp.zeros((32, 48), f32)
        back = jnp.zeros((32, 48), f32)
        for k in range(TAPS):
            ahead = jnp.where(shift == k, tap[k], ahead)
            back = jnp.where(shift == k, tap[TAPS - 1 - k], back)
        if index == 1:
            back = -descent * back
        back = back.astype(bf16)
        tabs[index] = dot(ahead.astype(bf16), here).astype(bf16)
        tabs[2 + index, :, 0:PAD_C] = dot(back, here[:, OFF_C:EXT]).astype(bf16)
        for d in range(8):
            n = REGIONS[d][3]
            coord = region_coords(d, n)[index]
            rim = jnp.where(iota((48, n), 0) == jnp.broadcast_to(coord, (48, n)), 1.0, 0.0).astype(bf16)
            back_tabs[index, d, :, 0:n] = dot(back, rim).astype(bf16)

    quality = jnp.zeros((SLOTS, LEV), f32)
    slot = iota((SLOTS, LEV), 0)
    for s in range(SLOTS):
        quality = jnp.where(slot == s, qual[0, 0, 0, s].astype(f32), quality)
    weights = jnp.where(slot < count[0, 0, 0], 0.5 * quality, 0.0)

    for c in ccopies:
        c.wait_recv()
    total = n_mem * SLOTS
    table_i, table_j = by_tile(jnp.concatenate([colall[o] for o in range(n_mem)], axis=0))
    row = iota((total, LEV), 0)
    spread_rows = one_hot(iota((total, 1), 0) >> 4, n_mem)
    lane = iota((total, LEV), 1)
    own_slot = lane == (row & 15)

    def along_rows(table):
        wide = dot(spread_rows, table.astype(f32).astype(bf16))
        return jnp.sum(jnp.where(own_slot, wide, 0.0), axis=1, keepdims=True)

    own_i, own_j = along_rows(table_i), along_rows(table_j)
    lanes = iota((total, 32), 1).astype(f32)
    pick_i = jnp.where(lanes == own_i, 1.0, 0.0).astype(bf16)
    pick_j = jnp.where(lanes == own_j, 1.0, 0.0).astype(bf16)
    for q in range(0, EXT, 128):
        part = dot(pick_i, tabs[0, :, q:q + 128]) * dot(pick_j, tabs[1, :, q:q + 128])
        w2[:, q:q + 128] = part.astype(bf16)

    acc[...] = dot(w2[:, OFF_C:EXT], xall[OFF_C:EXT, :])
    column = jnp.broadcast_to(TILE * own_i + own_j, (total, LEV))
    lane = lane.astype(f32)
    select = jnp.concatenate(
        [jnp.where(lane + float(q) == column, 1.0, 0.0).astype(bf16) for q in range(0, PAD_C, 128)], axis=1)
    ensobs[...] = dot(select, eall[OFF_C:EXT, :])
    for lo, hi, row, rows in GROUPS:
        recv_rims(xrims, lo, hi)
        acc[...] += dot(w2[:, row:row + rows], xall[row:row + rows, :])
    product = acc[...] * ensobs[...]
    part = product[:, 0:LEV]
    for m in range(1, MEM):
        part = part + product[:, m * LEV:(m + 1) * LEV]
    gsend[...] = part.astype(bf16)
    for c in gcopies:
        c.start()
    start_some(erims, (2, 3), True)
    grecv[mine, :] = gsend[mine, :]

    column_t = jnp.transpose(column)[0:1, :]
    cell = iota((CELLS, total), 0).astype(f32)
    st[...] = jnp.where(cell == jnp.broadcast_to(column_t, (CELLS, total)), 1.0, 0.0).astype(bf16)

    def build(b, _):
        rows = pl.ds(pl.multiple_of(b * 64, 64), 64)
        i, j = by_tile(iota((64, 1), 0) + b * 64)
        at_i, at_j = one_hot(i, 32), one_hot(j, 32)
        for q in range(0, PAD_C, 128):
            part = dot(at_i, tabs[2, :, q:q + 128]) * dot(at_j, tabs[3, :, q:q + 128])
            k2c[rows, q:q + 128] = part.astype(bf16)
        return 0
    lax.fori_loop(0, CELLS // 64, build, 0)
    for d in range(8):
        dz, dl, _, rows = REGIONS[d]
        r = iota((rows, 1), 0)
        i, j = by_tile(r) if dl == 0 else (r >> 3, r & 7)
        i, j = i + (TILE - HALF if dz == 1 else 0), j + (TILE - HALF if dl == 1 else 0)
        part = dot(one_hot(i, 32), back_tabs[0, d, :, 0:rows]) * dot(one_hot(j, 32), back_tabs[1, d, :, 0:rows])
        (k2z, k2l, k2x, k2x)[d // 2][d % 2 if d < 4 else d - 4] = part.astype(bf16)

    for c in gcopies:
        c.wait_recv()
    observed = jnp.zeros((SLOTS, LEV), f32)
    for o in range(n_mem):
        observed = observed + grecv[o * SLOTS:(o + 1) * SLOTS, :].astype(f32)
    residual = weights * (observed - vals[...])
    rall[mine, :] = residual.astype(bf16)
    for c in rcopies:
        c.start()
    start_some(erims, (4, 5, 6, 7), True)
    res_ref[...] = residual
    for m in range(MEM):
        out_ref[m] = (1.0 - descent) * ctrl[:, m * LEV:(m + 1) * LEV].reshape(TILE, TILE, LEV)
    for c in rcopies:
        c.wait_recv()

    adjoint = dot(st[...], rall[...])
    azs[...] = adjoint.astype(bf16)
    field = adjoint.reshape(TILE, TILE, LEV)
    for dz, dl, row, rows in REGIONS[2:]:
        astage[row - OFF_L:row - OFF_L + rows, :] = piece(dz, dl, field).astype(bf16)
    start_rims(arims)

    def weighted(row, rows, adj):
        wide = jnp.concatenate([adj] * MEM, axis=1)
        return (eall[row:row + rows, :].astype(f32) * wide).astype(bf16)

    zero = jnp.zeros((PAD_C - CELLS, LEV), f32)
    back = dot(k2c[...], weighted(OFF_C, PAD_C, jnp.concatenate([adjoint, zero], axis=0)))
    for m in range(MEM):
        out_ref[m] += back[:, m * LEV:(m + 1) * LEV].reshape(TILE, TILE, LEV)
    recv_rims(erims, 0, 8)
    for d in range(8):
        recv_rims(arims, d, d + 1)
        row, rows = REGIONS[d][2:]
        matrix = (k2z, k2l, k2x, k2x)[d // 2][d % 2 if d < 4 else d - 4]
        back = dot(matrix, weighted(row, rows, aall[row:row + rows, :].astype(f32)))
        for m in range(MEM):
            block = block_of(out_ref, m, d)
            block[...] += back[:, m * LEV:(m + 1) * LEV].reshape(block.shape)

    for copies in (xrims, erims, arims):
        sent_rims(copies)
    for copies in (ccopies, gcopies, rcopies):
        for c in copies:
            c.wait_send()


def write(a_ref, b_ref, a_out, b_out, sem):
    copies = [pltpu.make_async_copy(a_ref, a_out, sem.at[0]), pltpu.make_async_copy(b_ref, b_out, sem.at[1])]
    for c in copies:
        c.start()
    for c in copies:
        c.wait()


def shards(sizes, controls, ensemble, taps_lon, taps_lat, obs_columns, obs_count, obs_quality, obs_values):
    n_mem = sizes[2]
    total = n_mem * SLOTS
    vmem = pl.BlockSpec(memory_space=pltpu.VMEM)
    hbm = pl.BlockSpec(memory_space=pltpu.HBM)
    shapes = (jax.ShapeDtypeStruct((MEM, TILE, TILE, LEV), f32), jax.ShapeDtypeStruct((SLOTS, LEV), f32))
    results = pl.pallas_call(
        functools.partial(kernel, sizes),
        out_shape=shapes,
        in_specs=[hbm] * 5 + [pl.BlockSpec(memory_space=pltpu.SMEM)] + [hbm] * 2,
        out_specs=(vmem, vmem),
        scratch_shapes=[
            pltpu.VMEM((CELLS, WIDE), f32),
            pltpu.VMEM((EXT, WIDE), bf16),
            pltpu.VMEM((EXT, WIDE), bf16),
            pltpu.VMEM((EXT, LEV), bf16),
            pltpu.VMEM((OFF_C - OFF_L, WIDE), bf16),
            pltpu.VMEM((OFF_C - OFF_L, WIDE), bf16),
            pltpu.VMEM((CELLS, LEV), bf16),
            pltpu.VMEM((OFF_C - OFF_L, LEV), bf16),
            pltpu.VMEM((n_mem, 1, LEV), jnp.int32),
            pltpu.VMEM((total, LEV), bf16),
            pltpu.VMEM((total, LEV), bf16),
            pltpu.VMEM((total, LEV), bf16),
            pltpu.VMEM((total, EXT), bf16),
            pltpu.VMEM((CELLS, PAD_C), bf16),
            pltpu.VMEM((2, SIDE, SIDE), bf16),
            pltpu.VMEM((2, SIDE, SIDE), bf16),
            pltpu.VMEM((4, CORNER, CORNER), bf16),
            pltpu.VMEM((CELLS, total), bf16),
            pltpu.VMEM((4, 32, EXT), bf16),
            pltpu.VMEM((2, 8, 32, SIDE), bf16),
            pltpu.VMEM((total, WIDE), f32),
            pltpu.VMEM((total, WIDE), f32),
            pltpu.SMEM((TAPS,), f32),
            pltpu.SMEM((TAPS,), f32),
            pltpu.SMEM((1, 1, 1, SLOTS), jnp.int32),
            pltpu.SMEM((1, 1, 1, SLOTS), jnp.int32),
            pltpu.VMEM((SLOTS, LEV), f32),
            pltpu.SemaphoreType.DMA((2 * MEM,)),
            pltpu.SemaphoreType.DMA((5,)),
            pltpu.SemaphoreType.DMA((3, 8)),
            pltpu.SemaphoreType.DMA((3, 8)),
            pltpu.SemaphoreType.DMA((3, n_mem)),
            pltpu.SemaphoreType.DMA((3, n_mem)),
        ],
        compiler_params=pltpu.CompilerParams(collective_id=0, has_side_effects=True, vmem_limit_bytes=30 * 1024 * 1024),
        name="step",
    )(*[x if x.size == 1 else pltpu.with_memory_space_constraint(x, pltpu.HBM) for x in (
        controls.reshape(MEM, CELLS, LEV),
        ensemble.reshape(MEM, CELLS, LEV),
        taps_lon,
        taps_lat,
        obs_columns,
        obs_count,
        obs_quality,
        obs_values.reshape(SLOTS, LEV),
    )])
    new_controls, residual = pl.pallas_call(
        write,
        out_shape=shapes,
        in_specs=[pl.BlockSpec(memory_space=pl.ANY)] * 2,
        out_specs=(hbm, hbm),
        scratch_shapes=[pltpu.SemaphoreType.DMA((2,))],
        compiler_params=pltpu.CompilerParams(vmem_limit_bytes=1 << 20),
        name="write",
    )(*results)
    return new_controls, residual.reshape(obs_values.shape)


def solution(mesh):
    sizes = (mesh.shape["lon"], mesh.shape["lat"], mesh.shape["mem"])
    placed = (
        P("mem", "lon", "lat", None),
        P("mem", "lon", "lat", None),
        P(),
        P(),
        P("lon", "lat", "mem", None),
        P("lon", "lat", "mem"),
        P("lon", "lat", "mem", None),
        P("lon", "lat", "mem", None, None),
    )
    return jax.shard_map(
        functools.partial(shards, sizes),
        mesh=mesh,
        in_specs=placed,
        out_specs=(P("mem", "lon", "lat", None), P("lon", "lat", "mem", None, None)),
        check_vma=False,
    )
```

time: 56.8 us -> 51.9 us (0.914)
  other arithmetic: 2.76 us -> 0 us
  Pallas kernels: 51.9 us -> 50.5 us
  local copies, waits for them, and re-layouts: 0.6 us -> 0 us
    add x1 -> x0, other arithmetic: 2.76 us -> none  [shards(): new_controls = (1.0 - descent) * controls + step]
    pallas_call x1 -> x2, Pallas kernels: 51.9 us -> 50.5 us  [the longest x1 49.4 us: shards(): pl.pallas_call(functools.partial(kernel, sizes), out_shape=shapes, in_spe...]
    unnamed x3 -> x0, local copies, waits for them, and re-layouts: 0.6 us -> none
where the time goes in v2:
time: 51.9 us; the launch traced here: 51.7 us
  Pallas kernels  50.5 us (97%)
  between operations  1.29 us (2%)
    pallas_call x1, Pallas kernels, shards(): pl.pallas_call(functools.partial(kernel, sizes), out_shape=shapes, in_spe...  49.4 us

profile of v2, /device:TPU:1, one launch (start us, length us, event | category | flops | bytes accessed | tf_op | source)
XLA Modules:
  0.0 51.7 jit_solution(9982194897854642521)
XLA Ops:
  1.3 49.4 %step.1 = (f32[4,24,24,128]{3,2,1,0:T(8,128)S(1)}, f32[16,128]{1,0:T(8,128)S(1)}) custom-call(f32[4,576,128]{2,1,0:T(8,128)} %bitcast.4, bf16[4,576,128]{2,1,0:T(8,128)(2,1)} %bitcast.5, f32[17]{0:T(128)} %tlon_hbm.1, f32[17]{0:T(128)} %tlat_hbm.1, s32[1,1,1,16]{3,2,1,0:T(1,128)} %cols_hbm.1, s32[1,1,1]{2,1,0:T(1,128)S(6)} %copy.10.count, ...), custom_call_target="tpu_custom_call" | custom-call | tf_op jit(solution)/shard_map/step/pallas_call | solution.py:399
  50.7 1.0 %write.1 = (f32[4,24,24,128]{3,2,1,0:T(8,128)}, f32[16,128]{1,0:T(8,128)}) custom-call(f32[4,24,24,128]{3,2,1,0:T(8,128)S(1)} %get-tuple-element.6.a_ref, f32[16,128]{1,0:T(8,128)S(1)} %get-tuple-element.7.b_ref), custom_call_target="tpu_custom_call" | custom-call | tf_op jit(solution)/shard_map/write/pallas_call | solution.py:451

commit v3 on v2

--- a/solution.py
+++ b/solution.py
@@ -34,7 +34,7 @@
     (-1, 1, OFF_X + 2 * CORNER, CORNER),
     (1, 1, OFF_X + 3 * CORNER, CORNER),
 )
-GROUPS = ((0, 2, OFF_Z, 2 * SIDE), (2, 4, OFF_L, 2 * SIDE), (4, 8, OFF_X, 4 * CORNER))
+GROUPS = (((2, 3), OFF_L, 2 * SIDE), ((10, 11), OFF_Z, 2 * SIDE), ((4, 5, 6, 7), OFF_X, 4 * CORNER))
 MESH = pl.DeviceIdType.MESH
 f32 = jnp.float32
 bf16 = jnp.bfloat16
@@ -47,6 +47,12 @@
 def by_tile(q):
     i = (q * 2731) >> 16
     return i, q - TILE * i
+
+
+def strips(q):
+    strip = q >> 6
+    first = jnp.where(strip == 0, 0, jnp.where(strip == 1, TILE - HALF, HALF))
+    return (q & 63) >> 3, (q & 7) + first
 
 
 def column_coords():
@@ -55,7 +61,7 @@
         lon.append(i)
         lat.append(j)
     for base in (0, HALF + TILE):
-        i, j = by_tile(iota((1, SIDE), 1))
+        i, j = strips(iota((1, SIDE), 1))
         add(i + base, j + HALF)
     for base in (0, HALF + TILE):
         q = iota((1, SIDE), 1)
@@ -74,18 +80,35 @@
     return jnp.dot(a, b, preferred_element_type=f32)
 
 
-def piece(dz, dl, field):
+def lon_rim(rows):
+    field = rows.reshape(HALF, TILE, rows.shape[1])
+    parts = [field[:, j:j + HALF, :].reshape(CORNER, rows.shape[1]) for j in (0, TILE - HALF, HALF)]
+    return jnp.concatenate(parts, axis=0)
+
+
+def edge(dz, dl, field):
     i0, ni = {-1: (TILE - HALF, HALF), 1: (0, HALF), 0: (0, TILE)}[dz]
     j0 = {-1: TILE - HALF, 1: 0}[dl]
-    part = field[i0:i0 + ni, j0:j0 + HALF, :]
-    return part.reshape(ni * HALF, part.shape[2])
+    return field[i0:i0 + ni, j0:j0 + HALF, :].reshape(ni * HALF, field.shape[2])
+
+
+def stage_edges(stage, field, which):
+    n = field.shape[1]
+    for d in which:
+        dz, dl, row, rows = REGIONS[d]
+        if dl == 0:
+            first = CELLS - SIDE if dz == -1 else 0
+            value = lon_rim(field[first:first + SIDE, :])
+        else:
+            value = edge(dz, dl, field.reshape(TILE, TILE, n))
+        stage[row:row + rows, :] = value.astype(bf16)
 
 
 def region_coords(d, n):
     dz, dl, _, _ = REGIONS[d]
     start = {-1: 0, 0: HALF, 1: HALF + TILE}
     q = iota((1, n), 1)
-    i, j = by_tile(q) if dl == 0 else (q >> 3, q & 7)
+    i, j = strips(q) if dl == 0 else (q >> 3, q & 7)
     return i + start[dz], j + start[dl]
 
 
@@ -100,9 +123,9 @@
 
 
 def kernel(sizes, ctrl_hbm, ens_hbm, tlon_hbm, tlat_hbm, cols_hbm, count, qual_hbm, vals_hbm, out_ref, res_ref,
-           ctrl, xall, eall, aall, xstage, estage, azs, astage, colall, gsend, grecv, rall, w2, k2c, k2z, k2l, k2x, st, tabs,
+           ctrl, xall, eall, aall, xstage, estage, astage, colall, gsend, grecv, rall, w2, k2c, k2z, k2l, k2x, st, tabs,
            back_tabs, ensobs, acc, tlon, tlat, cols, qual, vals,
-           load_sem, small_sem, rim_send, rim_recv, mem_send, mem_recv):
+           load_sem, small_sem, rim_send, rim_recv, mem_send, mem_recv, far_sem):
     n_lon, n_lat, n_mem = sizes
     n_y = n_mem // 2
     z = lax.axis_index("lon")
@@ -131,21 +154,28 @@
         return lax.rem(my_x + dx, 2) * n_y + lax.rem(my_y + dy, n_y)
 
     barrier = pltpu.get_barrier_semaphore()
-    for dx, dy in steps:
+    near = [(dx, dy) for dx, dy in steps if min(dy, n_y - dy) <= 2]
+    for dx, dy in near:
         pl.semaphore_signal(barrier, inc=1, device_id={"mem": peer_of(dx, dy)}, device_id_type=MESH)
     for dz, dl, _, _ in REGIONS:
         def greet(dz=dz, dl=dl):
             pl.semaphore_signal(barrier, inc=1, device_id={"lon": lon_of(dz), "lat": l + dl}, device_id_type=MESH)
         guarded(has(dl), greet)
 
-    loads = [pltpu.make_async_copy(ctrl_hbm.at[m], ctrl.at[:, m * LEV:(m + 1) * LEV], load_sem.at[m]) for m in range(MEM)]
+    loads = []
+    for part, first in enumerate((0, CELLS - SIDE, SIDE)):
+        loads.append([
+            pltpu.make_async_copy(
+                ctrl_hbm.at[m, first:first + SIDE, :], ctrl.at[first:first + SIDE, m * LEV:(m + 1) * LEV], load_sem.at[part, m])
+            for m in range(MEM)
+        ])
     loads_e = [
-        pltpu.make_async_copy(ens_hbm.at[m], eall.at[OFF_C:OFF_C + CELLS, m * LEV:(m + 1) * LEV], load_sem.at[MEM + m])
+        pltpu.make_async_copy(ens_hbm.at[m], eall.at[OFF_C:OFF_C + CELLS, m * LEV:(m + 1) * LEV], load_sem.at[3, m])
         for m in range(MEM)
     ]
     pairs = ((cols_hbm, cols), (qual_hbm, qual), (tlon_hbm, tlon), (tlat_hbm, tlat), (vals_hbm, vals))
     small = [pltpu.make_async_copy(a, b, small_sem.at[k]) for k, (a, b) in enumerate(pairs)]
-    for c in loads + small + loads_e:
+    for c in loads[0] + loads[1] + loads[2] + small + loads_e:
         c.start()
 
     xall[OFF_C + CELLS:EXT, :] = jnp.zeros((64, WIDE), bf16)
@@ -159,6 +189,12 @@
             aall[row:row + SIDE, :] = jnp.zeros((SIDE, LEV), bf16)
             aall[xrow:xrow + 2 * CORNER, :] = jnp.zeros((2 * CORNER, LEV), bf16)
 
+    for part, (dz, dl, row, rows) in ((1, REGIONS[0]), (0, REGIONS[1])):
+        for c in loads[part]:
+            c.wait()
+        first = CELLS - SIDE if dz == -1 else 0
+        xstage[row:row + rows, :] = lon_rim(ctrl[first:first + SIDE, :]).astype(bf16)
+
     for c in small:
         c.wait()
     lane1 = iota((1, LEV), 1)
@@ -167,35 +203,45 @@
         col = jnp.where(lane1 == s, cols[0, 0, 0, s], col)
     colall[me] = col
 
-    for c in loads:
-        c.wait()
-    field = ctrl[...]
-    xall[OFF_C:OFF_C + CELLS, :] = field.astype(bf16)
-    field = field.reshape(TILE, TILE, WIDE)
-    for dz, dl, row, rows in REGIONS[2:]:
-        xstage[row - OFF_L:row - OFF_L + rows, :] = piece(dz, dl, field).astype(bf16)
-
-    both = jnp.where((l > 0) & (l < n_lat - 1), 8, 5)
-    pl.semaphore_wait(barrier, both + n_mem - 1)
-
-    def rim_copy(kind, d, own, own_row, stage, dst):
-        dz, dl, row, rows = REGIONS[d]
-        if dl == 0:
-            first = own_row + (CELLS - SIDE if dz == -1 else 0)
-            src = own.at[first:first + rows, :]
-        else:
-            src = stage.at[row - OFF_L:row - OFF_L + rows, :]
+    around = jnp.where((l > 0) & (l < n_lat - 1), 8, 5)
+    pl.semaphore_wait(barrier, around + len(near))
+
+    def rim_copy(kind, d, lo, hi, src, dst, sem, dz, dl):
+        row = REGIONS[d][2]
         return pltpu.make_async_remote_copy(
-            src_ref=src, dst_ref=dst.at[row:row + rows, :],
-            send_sem=rim_send.at[kind, d], recv_sem=rim_recv.at[kind, d],
+            src_ref=src, dst_ref=dst.at[row + lo:row + hi, :],
+            send_sem=rim_send.at[kind, sem], recv_sem=rim_recv.at[kind, sem],
             device_id={"lon": lon_of(-dz), "lat": l - dl}, device_id_type=MESH)
+
+    def rim_copies(kind, stage, dst):
+        made = []
+        for sem in range(12):
+            d = sem if sem < 8 else sem % 2
+            dz, dl, row, rows = REGIONS[d]
+            lo, hi = (CORNER * (max(sem - 6, 0) // 2), CORNER * (max(sem - 6, 0) // 2 + 1)) if d < 2 else (0, rows)
+            if d < 4:
+                src = stage.at[row + lo:row + hi, :]
+            else:
+                first = (OFF_Z if dz == -1 else OFF_Z + SIDE) + (CORNER if dl == -1 else 0)
+                src, dz = dst.at[first:first + CORNER, :], 0
+            made.append(rim_copy(kind, d, lo, hi, src, dst, sem, dz, dl))
+        return made
+
+    def adjoint_copies(stage, dst):
+        made = []
+        for d, (dz, dl, row, rows) in enumerate(REGIONS):
+            made.append(rim_copy(2, d, 0, rows, stage.at[row:row + rows, :], dst, d, dz, dl))
+        return made
 
     def crosses(d):
         return lax.rem(l, 2) == (1 if REGIONS[d][1] == -1 else 0)
 
-    def start_rims(copies):
-        for d, c in enumerate(copies):
-            guarded(has(-REGIONS[d][1]), c.start)
+    def lat_of(sem):
+        return REGIONS[sem][1] if sem < 8 else 0
+
+    def start_rims(copies, which):
+        for d in which:
+            guarded(has(-lat_of(d)), copies[d].start)
 
     def start_some(copies, which, across):
         for d in which:
@@ -207,13 +253,41 @@
                 far = crosses(d)
                 guarded(has(-dl) & (far if across else jnp.logical_not(far)), copies[d].start)
 
-    def recv_rims(copies, lo, hi):
-        for d in range(lo, hi):
-            guarded(has(REGIONS[d][1]), copies[d].wait_recv)
+    def recv_rims(copies, which):
+        for d in which:
+            guarded(has(lat_of(d)), copies[d].wait_recv)
 
     def sent_rims(copies):
         for d, c in enumerate(copies):
-            guarded(has(-REGIONS[d][1]), c.wait_send)
+            guarded(has(-lat_of(d)), c.wait_send)
+
+    def by_parity(odd, even):
+        pl.when(lax.rem(l, 2) == 1)(odd)
+        pl.when(lax.rem(l, 2) == 0)(even)
+
+    def send_strips(copies):
+        by_parity(lambda: start_rims(copies, (0, 1, 8, 9)), lambda: start_rims(copies, (8, 9, 0, 1)))
+
+    def pass_strips(copies, across):
+        def high(start):
+            recv_rims(copies, (8, 9))
+            if start:
+                start_rims(copies, (4, 5))
+
+        def low(start):
+            recv_rims(copies, (0, 1))
+            if start:
+                start_rims(copies, (6, 7))
+
+        def low_high():
+            low(True)
+            high(across)
+
+        def high_low():
+            high(True)
+            low(across)
+
+        by_parity(low_high, high_low)
 
     def rows_of(index):
         return pl.ds(pl.multiple_of(index * SLOTS, SLOTS), SLOTS)
@@ -230,23 +304,27 @@
                 device_id={"mem": peer}, device_id_type=MESH))
         return made
 
-    xrims = [rim_copy(0, d, xall, OFF_C, xstage, xall) for d in range(8)]
-    erims = [rim_copy(1, d, eall, OFF_C, estage, eall) for d in range(8)]
-    arims = [rim_copy(2, d, azs, 0, astage, aall) for d in range(8)]
+    xrims = rim_copies(0, xstage, xall)
+    erims = rim_copies(1, estage, eall)
+    arims = adjoint_copies(astage, aall)
     ccopies = mem_copies(0, lambda peer: colall.at[me], colall.at[me])
     gcopies = mem_copies(1, lambda peer: gsend.at[rows_of(peer), :], grecv.at[mine, :])
     rcopies = mem_copies(2, lambda peer: rall.at[mine, :], rall.at[mine, :])
 
-    for c in ccopies:
-        c.start()
-    start_rims(xrims)
-
-    for c in loads_e:
+    far = [(0, 2), (0, n_y - 2)] if len(near) < len(steps) else []
+    for dx, dy in far:
+        pl.semaphore_signal(far_sem, inc=1, device_id={"mem": peer_of(dx, dy)}, device_id_type=MESH)
+    for d in range(4, 8):
+        dz, dl, row, rows = REGIONS[d]
+        first = (OFF_Z if dz == -1 else OFF_Z + SIDE) + (CORNER if dl == -1 else 0)
+        corner = rim_copy(0, d, 0, rows, xstage.at[first:first + rows, :], xall, d, dz, dl)
+        guarded(has(-dl) & crosses(d), corner.start)
+    send_strips(xrims)
+    start_rims(xrims, (10, 11))
+    for c in loads[2]:
         c.wait()
-    field = eall[OFF_C:OFF_C + CELLS, :].astype(f32).reshape(TILE, TILE, WIDE)
-    for dz, dl, row, rows in REGIONS[2:]:
-        estage[row - OFF_L:row - OFF_L + rows, :] = piece(dz, dl, field).astype(bf16)
-    start_some(erims, range(8), False)
+    stage_edges(xstage, ctrl[...], (2, 3))
+    start_rims(xrims, (2, 3))
 
     shift = iota((32, 48), 1) - iota((32, 48), 0)
     for index, (tap, coord) in enumerate(zip((tlon, tlat), column_coords())):
@@ -267,6 +345,18 @@
             rim = jnp.where(iota((48, n), 0) == jnp.broadcast_to(coord, (48, n)), 1.0, 0.0).astype(bf16)
             back_tabs[index, d, :, 0:n] = dot(back, rim).astype(bf16)
 
+    if far:
+        pl.semaphore_wait(far_sem, len(far))
+    for c in ccopies:
+        c.start()
+    pass_strips(xrims, False)
+    for c in loads_e:
+        c.wait()
+    stage_edges(estage, eall[OFF_C:OFF_C + CELLS, :].astype(f32), range(4))
+    start_rims(erims, (0, 1, 8, 9, 10, 11))
+    start_some(erims, (2, 3), False)
+    xall[OFF_C:OFF_C + CELLS, :] = ctrl[...].astype(bf16)
+
     quality = jnp.zeros((SLOTS, LEV), f32)
     slot = iota((SLOTS, LEV), 0)
     for s in range(SLOTS):
@@ -300,8 +390,8 @@
     select = jnp.concatenate(
         [jnp.where(lane + float(q) == column, 1.0, 0.0).astype(bf16) for q in range(0, PAD_C, 128)], axis=1)
     ensobs[...] = dot(select, eall[OFF_C:EXT, :])
-    for lo, hi, row, rows in GROUPS:
-        recv_rims(xrims, lo, hi)
+    for which, row, rows in GROUPS:
+        recv_rims(xrims, which)
         acc[...] += dot(w2[:, row:row + rows], xall[row:row + rows, :])
     product = acc[...] * ensobs[...]
     part = product[:, 0:LEV]
@@ -343,43 +433,39 @@
     rall[mine, :] = residual.astype(bf16)
     for c in rcopies:
         c.start()
-    start_some(erims, (4, 5, 6, 7), True)
+    pass_strips(erims, True)
     res_ref[...] = residual
     for m in range(MEM):
         out_ref[m] = (1.0 - descent) * ctrl[:, m * LEV:(m + 1) * LEV].reshape(TILE, TILE, LEV)
+    sent_rims(xrims)
+    for c in ccopies + gcopies:
+        c.wait_send()
     for c in rcopies:
         c.wait_recv()
 
     adjoint = dot(st[...], rall[...])
-    azs[...] = adjoint.astype(bf16)
-    field = adjoint.reshape(TILE, TILE, LEV)
-    for dz, dl, row, rows in REGIONS[2:]:
-        astage[row - OFF_L:row - OFF_L + rows, :] = piece(dz, dl, field).astype(bf16)
-    start_rims(arims)
-
-    def weighted(row, rows, adj):
-        wide = jnp.concatenate([adj] * MEM, axis=1)
-        return (eall[row:row + rows, :].astype(f32) * wide).astype(bf16)
+    stage_edges(astage, adjoint, range(8))
+    start_rims(arims, (4, 5, 6, 7, 2, 3, 0, 1))
 
     zero = jnp.zeros((PAD_C - CELLS, LEV), f32)
-    back = dot(k2c[...], weighted(OFF_C, PAD_C, jnp.concatenate([adjoint, zero], axis=0)))
+    wide = jnp.concatenate([jnp.concatenate([adjoint, zero], axis=0)] * MEM, axis=1)
+    back = dot(k2c[...], (eall[OFF_C:EXT, :].astype(f32) * wide).astype(bf16))
     for m in range(MEM):
         out_ref[m] += back[:, m * LEV:(m + 1) * LEV].reshape(TILE, TILE, LEV)
-    recv_rims(erims, 0, 8)
-    for d in range(8):
-        recv_rims(arims, d, d + 1)
+    recv_rims(erims, (2, 3, 4, 5, 6, 7, 10, 11))
+    sent_rims(erims)
+    for c in rcopies:
+        c.wait_send()
+    for d in (2, 3, 0, 1, 4, 5, 6, 7):
+        recv_rims(arims, (d,))
         row, rows = REGIONS[d][2:]
         matrix = (k2z, k2l, k2x, k2x)[d // 2][d % 2 if d < 4 else d - 4]
-        back = dot(matrix, weighted(row, rows, aall[row:row + rows, :].astype(f32)))
+        back = dot(matrix, eall[row:row + rows, :] * jnp.concatenate([aall[row:row + rows, :]] * MEM, axis=1))
         for m in range(MEM):
             block = block_of(out_ref, m, d)
             block[...] += back[:, m * LEV:(m + 1) * LEV].reshape(block.shape)
 
-    for copies in (xrims, erims, arims):
-        sent_rims(copies)
-    for copies in (ccopies, gcopies, rcopies):
-        for c in copies:
-            c.wait_send()
+    sent_rims(arims)
 
 
 def write(a_ref, b_ref, a_out, b_out, sem):
@@ -406,10 +492,9 @@
             pltpu.VMEM((EXT, WIDE), bf16),
             pltpu.VMEM((EXT, WIDE), bf16),
             pltpu.VMEM((EXT, LEV), bf16),
-            pltpu.VMEM((OFF_C - OFF_L, WIDE), bf16),
-            pltpu.VMEM((OFF_C - OFF_L, WIDE), bf16),
-            pltpu.VMEM((CELLS, LEV), bf16),
-            pltpu.VMEM((OFF_C - OFF_L, LEV), bf16),
+            pltpu.VMEM((OFF_X, WIDE), bf16),
+            pltpu.VMEM((OFF_X, WIDE), bf16),
+            pltpu.VMEM((OFF_C, LEV), bf16),
             pltpu.VMEM((n_mem, 1, LEV), jnp.int32),
             pltpu.VMEM((total, LEV), bf16),
             pltpu.VMEM((total, LEV), bf16),
@@ -429,12 +514,13 @@
             pltpu.SMEM((1, 1, 1, SLOTS), jnp.int32),
             pltpu.SMEM((1, 1, 1, SLOTS), jnp.int32),
             pltpu.VMEM((SLOTS, LEV), f32),
-            pltpu.SemaphoreType.DMA((2 * MEM,)),
+            pltpu.SemaphoreType.DMA((4, MEM)),
             pltpu.SemaphoreType.DMA((5,)),
-            pltpu.SemaphoreType.DMA((3, 8)),
-            pltpu.SemaphoreType.DMA((3, 8)),
+            pltpu.SemaphoreType.DMA((3, 12)),
+            pltpu.SemaphoreType.DMA((3, 12)),
             pltpu.SemaphoreType.DMA((3, n_mem)),
             pltpu.SemaphoreType.DMA((3, n_mem)),
+            pltpu.SemaphoreType.REGULAR,
         ],
         compiler_params=pltpu.CompilerParams(collective_id=0, has_side_effects=True, vmem_limit_bytes=30 * 1024 * 1024),
         name="step",

time: 51.9 us -> 51.6 us (level)
  no operation moved by 1% of the time
where the time goes in v3:
time: 51.6 us; the launch traced here: 51.4 us
  Pallas kernels  50.2 us (97%)
  between operations  1.29 us (2%)
    pallas_call x1, Pallas kernels, shards(): pl.pallas_call(functools.partial(kernel, sizes), out_shape=shapes, in_spe...  49.1 us
    pallas_call x1, Pallas kernels, shards(): pl.pallas_call(write, out_shape=shapes, in_specs=[pl.BlockSpec(memory_spa...  1.03 us

profile of v3, /device:TPU:1, one launch (start us, length us, event | category | flops | bytes accessed | tf_op | source)
XLA Modules:
  0.0 51.4 jit_solution(12834846171214140843)
XLA Ops:
  1.3 49.1 %step.1 = (f32[4,24,24,128]{3,2,1,0:T(8,128)S(1)}, f32[16,128]{1,0:T(8,128)S(1)}) custom-call(f32[4,576,128]{2,1,0:T(8,128)} %bitcast.4, bf16[4,576,128]{2,1,0:T(8,128)(2,1)} %bitcast.5, f32[17]{0:T(128)} %tlon_hbm.1, f32[17]{0:T(128)} %tlat_hbm.1, s32[1,1,1,16]{3,2,1,0:T(1,128)} %cols_hbm.1, s32[1,1,1]{2,1,0:T(1,128)S(6)} %copy.10.count, ...), custom_call_target="tpu_custom_call" | custom-call | tf_op jit(solution)/shard_map/step/pallas_call | solution.py:485
  50.4 1.0 %write.1 = (f32[4,24,24,128]{3,2,1,0:T(8,128)}, f32[16,128]{1,0:T(8,128)}) custom-call(f32[4,24,24,128]{3,2,1,0:T(8,128)S(1)} %get-tuple-element.6.a_ref, f32[16,128]{1,0:T(8,128)S(1)} %get-tuple-element.7.b_ref), custom_call_target="tpu_custom_call" | custom-call | tf_op jit(solution)/shard_map/write/pallas_call | solution.py:537

commit v4 on v3

--- a/solution.py
+++ b/solution.py
@@ -266,28 +266,26 @@
         pl.when(lax.rem(l, 2) == 0)(even)
 
     def send_strips(copies):
-        by_parity(lambda: start_rims(copies, (0, 1, 8, 9)), lambda: start_rims(copies, (8, 9, 0, 1)))
-
-    def pass_strips(copies, across):
-        def high(start):
+        by_parity(lambda: start_rims(copies, (8, 9, 0, 1)), lambda: start_rims(copies, (0, 1, 8, 9)))
+
+    def pass_strips(copies):
+        def high():
             recv_rims(copies, (8, 9))
-            if start:
-                start_rims(copies, (4, 5))
-
-        def low(start):
+            start_rims(copies, (4, 5))
+
+        def low():
             recv_rims(copies, (0, 1))
-            if start:
-                start_rims(copies, (6, 7))
+            start_rims(copies, (6, 7))
+
+        def high_low():
+            high()
+            low()
 
         def low_high():
-            low(True)
-            high(across)
-
-        def high_low():
-            high(True)
-            low(across)
-
-        by_parity(low_high, high_low)
+            low()
+            high()
+
+        by_parity(high_low, low_high)
 
     def rows_of(index):
         return pl.ds(pl.multiple_of(index * SLOTS, SLOTS), SLOTS)
@@ -314,11 +312,6 @@
     far = [(0, 2), (0, n_y - 2)] if len(near) < len(steps) else []
     for dx, dy in far:
         pl.semaphore_signal(far_sem, inc=1, device_id={"mem": peer_of(dx, dy)}, device_id_type=MESH)
-    for d in range(4, 8):
-        dz, dl, row, rows = REGIONS[d]
-        first = (OFF_Z if dz == -1 else OFF_Z + SIDE) + (CORNER if dl == -1 else 0)
-        corner = rim_copy(0, d, 0, rows, xstage.at[first:first + rows, :], xall, d, dz, dl)
-        guarded(has(-dl) & crosses(d), corner.start)
     send_strips(xrims)
     start_rims(xrims, (10, 11))
     for c in loads[2]:
@@ -349,7 +342,7 @@
         pl.semaphore_wait(far_sem, len(far))
     for c in ccopies:
         c.start()
-    pass_strips(xrims, False)
+    pass_strips(xrims)
     for c in loads_e:
         c.wait()
     stage_edges(estage, eall[OFF_C:OFF_C + CELLS, :].astype(f32), range(4))
@@ -433,7 +426,7 @@
     rall[mine, :] = residual.astype(bf16)
     for c in rcopies:
         c.start()
-    pass_strips(erims, True)
+    pass_strips(erims)
     res_ref[...] = residual
     for m in range(MEM):
         out_ref[m] = (1.0 - descent) * ctrl[:, m * LEV:(m + 1) * LEV].reshape(TILE, TILE, LEV)

time: 51.6 us -> 51.4 us (level)
  no operation moved by 1% of the time
where the time goes in v4:
time: 51.4 us; the launch traced here: 51.2 us
  Pallas kernels  49.9 us (97%)
  between operations  1.29 us (3%)
    pallas_call x1, Pallas kernels, shards(): pl.pallas_call(functools.partial(kernel, sizes), out_shape=shapes, in_spe...  48.9 us
    pallas_call x1, Pallas kernels, shards(): pl.pallas_call(write, out_shape=shapes, in_specs=[pl.BlockSpec(memory_spa...  1.03 us

profile of v4, /device:TPU:1, one launch (start us, length us, event | category | flops | bytes accessed | tf_op | source)
XLA Modules:
  0.0 51.2 jit_solution(12956946832987724617)
XLA Ops:
  1.3 48.9 %step.1 = (f32[4,24,24,128]{3,2,1,0:T(8,128)S(1)}, f32[16,128]{1,0:T(8,128)S(1)}) custom-call(f32[4,576,128]{2,1,0:T(8,128)} %bitcast.4, bf16[4,576,128]{2,1,0:T(8,128)(2,1)} %bitcast.5, f32[17]{0:T(128)} %tlon_hbm.1, f32[17]{0:T(128)} %tlat_hbm.1, s32[1,1,1,16]{3,2,1,0:T(1,128)} %cols_hbm.1, s32[1,1,1]{2,1,0:T(1,128)S(6)} %copy.10.count, ...), custom_call_target="tpu_custom_call" | custom-call | tf_op jit(solution)/shard_map/step/pallas_call | solution.py:478
  50.2 1.0 %write.1 = (f32[4,24,24,128]{3,2,1,0:T(8,128)}, f32[16,128]{1,0:T(8,128)}) custom-call(f32[4,24,24,128]{3,2,1,0:T(8,128)S(1)} %get-tuple-element.6.a_ref, f32[16,128]{1,0:T(8,128)S(1)} %get-tuple-element.7.b_ref), custom_call_target="tpu_custom_call" | custom-call | tf_op jit(solution)/shard_map/write/pallas_call | solution.py:530
